TPU v7x, 32 devices: a whole 2x2x4 slice. The times are simulated.
32 devices in a mesh: ctx: 8 (over z, y), grp: 2 (over core), head: 2 (over x).
Axes of the slice: x: 2, y: 2, z: 4, core: 2. Of those that a mesh axis runs over, the one named last changes fastest.
Arguments:
- residual: bfloat16 [2048, 2880], P(('ctx', 'grp')), may hold values from -10 to 10
- queries: bfloat16 [2048, 2048], P(('ctx', 'grp'), 'head'), may hold values from -32 to 32
- keys: bfloat16 [2048, 256], P(('ctx', 'grp'), 'head'), may hold values from -32 to 32
- values: bfloat16 [2048, 256], P(('ctx', 'grp'), 'head'), may hold values from -12 to 12
- out_weight: bfloat16 [2048, 2880], P('head'), may hold values from -0.125 to 0.125
- norm_gain: float32 [2880], replicated, may hold values from 0.5 to 1.5
- routes: int32 [2048, 4], P(('ctx', 'grp')), may hold values from 0 to 7, all different within a row; in each aligned block of 128 rows (0 to 127, 128 to 255, ...) at most 72 rows name the same one
- expert_weight: bfloat16 [8, 2880, 2, 1536], P('ctx', None, None, 'head'), may hold values from -0.109375 to 0.109375
Outputs:
- hidden: bfloat16 [2048, 2880], P(('ctx', 'grp'), 'head')
- active: bfloat16 [8, 2, 576, 1536], P('ctx', 'grp', None, 'head')
Inputs may be any that keep to these rules, and one draw needn't show every extreme that they name: `routes`: each token names 4 different experts; the 128 rows of one device name any one expert at most 72 times.
All inputs are finite; a program needn't handle non-finite values.
Results may differ from a plain program's by a relative error of at most 0.017.
Values may be sent and summed in bfloat16 or wider, within the bound.
A program may use at most 128 MiB of HBM per device.

v0:
```python
import jax
import jax.numpy as jnp
from jax import lax
from jax.sharding import PartitionSpec as P

D = 2880
HD = 64
TOP = 4


def shifted(value, axis, by):
    count = lax.axis_size(axis)
    pairs = [(i, i + by) for i in range(count) if 0 <= i + by < count]
    return lax.ppermute(value, axis, pairs)


def attend_block(running, query_heads, key_block, value_block, query_place, key_place, band):
    allowed = (
        (key_place[None, :] <= query_place[:, None])
        & (query_place[:, None] - key_place[None, :] < band)
        & (key_place[None, :] >= 0)
    )

    def attend_live(carried):
        row_max, row_total, summed = carried
        scores = jnp.einsum(
            "tkgd,skd->kgts", query_heads, key_block, preferred_element_type=jnp.float32
        )
        scores = jnp.where(allowed, scores * query_heads.shape[-1] ** (-0.5), -1e30)
        new_max = jnp.maximum(row_max, jnp.max(scores, axis=-1))
        weights = jnp.where(allowed, jnp.exp(scores - new_max[..., None]), 0.0)
        factor = jnp.exp(row_max - new_max)
        row_total = row_total * factor + jnp.sum(weights, axis=-1)
        summed = summed * factor[..., None] + jnp.einsum(
            "kgts,skd->kgtd",
            weights.astype(jnp.bfloat16),
            value_block,
            preferred_element_type=jnp.float32,
        )
        return (new_max, row_total, summed)

    def skip_block(carried):
        return carried

    return lax.cond(jnp.any(allowed), attend_live, skip_block, running)


def finish_rows(gate_up, squares, hidden_width):
    inverse_rms = lax.rsqrt(squares / D + 1e-05)
    gate_part = gate_up[..., :hidden_width] * inverse_rms[..., None]
    up_part = gate_up[..., hidden_width:] * inverse_rms[..., None]
    return (gate_part * jax.nn.sigmoid(1.702 * gate_part) * (up_part + 1.0)).astype(jnp.bfloat16)


def body(residual, queries, keys, values, out_weight, norm_gain, routes, expert_weight):
    tokens_here = queries.shape[0]
    kv_local = keys.shape[1] // HD
    per_group = queries.shape[1] // keys.shape[1]
    query_heads = queries.reshape(tokens_here, kv_local, per_group, HD)
    ctx_index = lax.axis_index("ctx")
    grp_index = lax.axis_index("grp")
    head_index = lax.axis_index("head")
    heads_count = lax.axis_size("head")
    block_len = tokens_here * lax.axis_size("grp")
    reach_steps = max(1, lax.axis_size("ctx") // 16)
    band = reach_steps * block_len
    query_place = (
        ctx_index * block_len + grp_index * tokens_here + jnp.arange(tokens_here, dtype=jnp.int32)
    )
    own_keys, own_values = (
        lax.all_gather(keys, "grp", axis=0, tiled=True),
        lax.all_gather(values, "grp", axis=0, tiled=True),
    )

    def attend_from(running, key_flat, value_flat, distance):
        key_place = (ctx_index - distance) * block_len + jnp.arange(block_len, dtype=jnp.int32)
        return attend_block(
            running,
            query_heads,
            key_flat.reshape(block_len, kv_local, HD),
            value_flat.reshape(block_len, kv_local, HD),
            query_place,
            key_place,
            band,
        )

    running = (
        jnp.full((kv_local, per_group, tokens_here), -1e30, jnp.float32),
        jnp.zeros((kv_local, per_group, tokens_here), jnp.float32),
        jnp.zeros((kv_local, per_group, tokens_here, HD), jnp.float32),
    )
    running = attend_from(running, own_keys, own_values, 0)

    def cycle_turn(distance, carried):
        running, key_flat, value_flat = carried
        key_flat, value_flat = shifted((key_flat, value_flat), "ctx", 1)
        running = attend_from(running, key_flat, value_flat, distance)
        return (running, key_flat, value_flat)

    running = lax.fori_loop(1, reach_steps + 1, cycle_turn, (running, own_keys, own_values))[0]
    row_max, row_total, summed = running
    mixed = summed / row_total[..., None]
    attended = (
        jnp.transpose(mixed, (2, 0, 1, 3))
        .reshape(tokens_here, kv_local * per_group * HD)
        .astype(jnp.bfloat16)
    )
    partial_value = jnp.dot(attended, out_weight, preferred_element_type=jnp.float32)
    column_width = D // heads_count
    experts_all = expert_weight.shape[0] * lax.axis_size("ctx")
    routed = tokens_here * TOP
    capacity = min(tokens_here, routed // experts_all + max(1, routed // (8 * experts_all)))
    flat_routes = routes.reshape(routed)
    expert_hits = (
        flat_routes[:, None] == jnp.arange(experts_all, dtype=jnp.int32)[None, :]
    ).astype(jnp.bfloat16)
    earlier = jnp.tril(jnp.ones((routed, routed), jnp.bfloat16), -1)
    before = jnp.dot(earlier, expert_hits, preferred_element_type=jnp.float32)
    slot_index = jnp.sum(before * expert_hits.astype(jnp.float32), axis=1).astype(jnp.int32)
    hidden_width = expert_weight.shape[3]
    local_weight = expert_weight[0].reshape(D, 2 * hidden_width)
    projected = lax.psum_scatter(
        partial_value.astype(jnp.bfloat16), "head", scatter_dimension=1, tiled=True
    ).astype(jnp.float32)
    own_residual = lax.dynamic_slice_in_dim(residual, head_index * column_width, column_width, 1)
    hidden = (own_residual.astype(jnp.float32) + projected).astype(jnp.bfloat16)
    dest_index = flat_routes * capacity + slot_index
    route_rows = jnp.repeat(hidden, TOP, axis=0)
    outgoing = (
        jnp.zeros((experts_all * capacity, column_width), jnp.bfloat16)
        .at[dest_index]
        .set(route_rows)
    )
    arrived = lax.all_to_all(
        outgoing.reshape(experts_all, capacity, column_width),
        "ctx",
        split_axis=0,
        concat_axis=1,
        tiled=True,
    )
    arrived_rows = arrived.reshape(-1, column_width)
    slot_total = arrived_rows.shape[0]
    widened = lax.all_gather(arrived_rows, "head", axis=1, tiled=True).astype(jnp.float32)
    scaled = (widened * norm_gain[None, :]).astype(jnp.bfloat16)
    gate_up = jnp.dot(scaled, local_weight, preferred_element_type=jnp.float32)
    squares = jnp.sum(widened * widened, axis=1)
    gate_up, squares = (gate_up, squares)
    active = finish_rows(gate_up, squares, hidden_width)
    return (hidden, active.reshape(1, 1, slot_total, hidden_width))


def solution(mesh):
    in_specs = (
        P(("ctx", "grp"), None),
        P(("ctx", "grp"), "head"),
        P(("ctx", "grp"), "head"),
        P(("ctx", "grp"), "head"),
        P("head", None),
        P(),
        P(("ctx", "grp"), None),
        P("ctx", None, None, "head"),
    )
    out_specs = (P(("ctx", "grp"), "head"), P("ctx", "grp", None, "head"))
    return jax.shard_map(body, mesh=mesh, in_specs=in_specs, out_specs=out_specs, check_vma=False)
```

profile of v0, /device:TPU:0, one launch (start us, length us, event | category | flops | bytes accessed | tf_op | source)
XLA Modules:
  0.0 196.8 jit_solution(11392658521346276499)
XLA Ops:
  7.2 0.0 reduce-scatter.2.cloned.1.call-start
  7.2 0.9 copy.35
  8.1 2.2 %all_gather.9 = bf16[256,128]{0,1:T(8,128)(2,1)} all-gather(bf16[128,128]{0,1:T(8,128)(2,1)S(1)} %copy.35), channel_id=1, replica_groups=mesh['ctx'=8,'grp'=2,'head'=2] {'grp'}, dimensions={0}, use_global_device_ids=true | all-gather | bytes 98304 | tf_op jit(solution)/shard_map/all_gather | solution.py:71
  10.2 4.7 %collective-permute-start = (bf16[256,128]{0,1:T(8,128)(2,1)}, bf16[256,128]{0,1:T(8,128)(2,1)S(1)}, u32[]{:S(2)}, u32[]{:S(2)}) collective-permute-start(bf16[256,128]{0,1:T(8,128)(2,1)} %all_gather.9), channel_id=1, source_target_pairs={{0,4},{4,8},{8,12},{12,16},{16,20},{20,24},{24,28},{1,5},{5,9},{9,... | collective-permute-start | bytes 196616 | tf_op jit(solution)/shard_map/while/body/eval_jaxpr/ppermute | solution.py:14
  15.0 0.9 copy.37
  15.9 2.0 %all_gather.10 = bf16[256,128]{0,1:T(8,128)(2,1)} all-gather(bf16[128,128]{0,1:T(8,128)(2,1)S(1)} %copy.37), channel_id=1, replica_groups=mesh['ctx'=8,'grp'=2,'head'=2] {'grp'}, dimensions={0}, use_global_device_ids=true | all-gather | bytes 98304 | tf_op jit(solution)/shard_map/all_gather | solution.py:72
  17.9 3.4 %collective-permute-start.1 = (bf16[256,128]{0,1:T(8,128)(2,1)}, bf16[256,128]{0,1:T(8,128)(2,1)S(1)}, u32[]{:S(2)}, u32[]{:S(2)}) collective-permute-start(bf16[256,128]{0,1:T(8,128)(2,1)} %all_gather.10), channel_id=1, source_target_pairs={{0,4},{4,8},{8,12},{12,16},{16,20},{20,24},{24,28},{1,5},{5,9},{9,... | collective-permute-start | bytes 196616 | tf_op jit(solution)/shard_map/while/body/eval_jaxpr/ppermute | solution.py:14
  21.4 0.8 fusion.45
  22.2 1.1 copy.36
  24.6 5.3 %conditional.2 = (f32[2,8,128]{2,1,0:T(8,128)}, f32[2,8,128]{2,1,0:T(8,128)S(1)}, f32[2,8,128,64]{2,3,1,0:T(8,128)S(1)}) conditional(s32[]{:T(128)} %convert_element_type.65, () %tuple.30, (pred[128,256]{0,1:T(8,128)(4,1)S(1)}, bf16[256,128]{0,1:T(8,128)(2,1)}, bf16[128,2,8,64]{0,3,2,1:T(8,128)(2,1)S(1)}, bf16[256,128]{0,1:T(8,128)(2,1)}) %tuple.54), branch_computations={%region_2.3_spmd, %region_3.6_spmd} | conditional | flops 141172736 | bytes 7397400 | solution.py:45
  24.6 1.3 fusion
  26.0 0.6 exponential_multiply_fusion
  26.6 1.4 convolution_add_fusion
  28.0 1.2 fusion.2
  29.2 0.7 fusion.11
  29.9 0.0 collective-permute-done
  29.9 0.0 collective-permute-done.1
  30.0 0.1 divide_convert_fusion
  30.0 0.0 copy-start.3
  30.0 5.2 %convolution_convert_fusion = bf16[128,2880]{0,1:T(8,128)(2,1)} fusion(bf16[1024,2880]{0,1:T(8,128)(2,1)} %param.16, bf16[128,1024]{0,1:T(8,128)(2,1)S(1)} %bitcast.76), kind=kOutput, calls=%fused_computation.34 | convolution fusion | flops 755343360 | bytes 6897664 | tf_op jit(solution)/shard_map/dot_general | solution.py:108
  35.3 0.0 copy-start.2
  35.3 0.0 reduce-scatter.2.cloned.1.call-update
  35.3 0.0 all-gather.3.cloned.1.call-start
  35.4 0.0 copy-done.3
  35.4 0.1 copy.39
  35.5 0.1 eq.15
  35.6 0.3 fusion.28
  36.0 0.1 copy.38
  36.1 0.1 mul.108
  36.2 19.5 %reduce-scatter.2.cloned.1.call-done = bf16[128,1440]{0,1:T(8,128)(2,1)} async-done(((bf16[128,2880]{0,1:T(8,128)(2,1)}), bf16[128,1440]{0,1:T(8,128)(2,1)}) %reduce-scatter.2.cloned.1.call-update) | async-done | bytes 368656 | tf_op jit(solution)/shard_map/reduce_scatter | solution.py:122
  55.7 0.0 copy-done.2
  55.7 1.1 add_convert_fusion
  56.8 0.0 copy-start.1
  56.8 0.7 copy-done.1
  57.6 0.2 copy.40
  57.8 0.4 broadcast_in_dim.79
  58.2 0.8 reshape.122
  59.0 3.5 %scatter_custom_fusion = bf16[576,1440]{1,0:T(8,128)(2,1)S(1)} fusion(s32[512]{0:T(512)S(1)} %bitcast.79, bf16[512,1440]{1,0:T(8,128)(2,1)S(1)} %reshape.122, bf16[]{:T(256)} %constant.49.clone.1), kind=kCustom, calls=%fused_computation.46 | custom fusion | bytes 1658882 | tf_op jit(solution)/shard_map/scatter | solution.py:132
  62.5 46.6 %all_to_all.4 = bf16[8,72,1440]{2,1,0:T(8,128)(2,1)} all-to-all(bf16[8,72,1440]{2,1,0:T(8,128)(2,1)S(1)} %bitcast.73), channel_id=1, replica_groups=mesh['ctx'=8,'grp'=2,'head'=2] {'ctx'}, dimensions={0} | all-to-all | bytes 3317760 | tf_op jit(solution)/shard_map/all_to_all | solution.py:134
  109.1 0.0 all-gather.3.cloned.1.call-update
  109.1 9.0 %copy.48 = bf16[360,8,2,768]{3,1,2,0:T(8,128)(2,1)} copy(bf16[360,8,2,768]{3,2,1,0:T(2,128)(2,1)} %bitcast.70) | data formatting | bytes 17694720
  118.1 38.5 %all-gather.3.cloned.1.call-done = bf16[2,1440,576]{1,2,0:T(8,128)(2,1)} async-done(((bf16[1,1440,576]{1,2,0:T(8,128)(2,1)}), bf16[2,1440,576]{1,2,0:T(8,128)(2,1)}) %all-gather.3.cloned.1.call-update) | async-done | bytes 3317776 | tf_op jit(solution)/shard_map/all_gather | solution.py:143
  156.5 8.6 %copy.41 = f32[2,1440,576]{1,0,2:T(2,128)} copy(bf16[2,1440,576]{1,2,0:T(8,128)(2,1)} %all-gather.3.cloned.1.call-done) | data formatting | bytes 9953280 | tf_op jit(solution)/shard_map/convert_element_type | solution.py:143
  165.1 10.2 %reshape.128 = f32[2880,576]{0,1:T(8,128)} reshape(f32[2,1440,576]{1,0,2:T(2,128)} %copy.41) | data formatting | bytes 13271040 | tf_op jit(solution)/shard_map/convert_element_type | solution.py:143
  175.3 0.0 copy-start
  175.3 0.0 copy-start.4
  175.3 3.6 %multiply_reduce_fusion = f32[576]{0:T(1024)S(1)} fusion(f32[2880,576]{0,1:T(8,128)} %reshape.128), kind=kLoop, calls=%fused_computation.32 | loop fusion | flops 3317184 | bytes 6637824 | tf_op jit(solution)/shard_map/reduce_sum | solution.py:146
  178.9 1.2 copy-done
  180.2 0.0 copy-done.4
  180.2 8.2 %fusion.23 = f32[576,1536]{1,0:T(8,128)S(1)} fusion(bf16[2880,1536]{1,0:T(8,128)(2,1)} %bitcast.71, f32[2880,576]{0,1:T(8,128)S(1)} %copy-done, f32[2880]{0:T(1024)S(1)} %copy-done.4), kind=kOutput, calls=%fused_computation.35 | convolution fusion | flops 5099397120 | bytes 19033344 | tf_op jit(solution)/shard_map/dot_general | solution.py:145
  188.4 1.6 fusion.32
  (9 shorter events, 0.1 us)
Async XLA Ops:
  7.2 48.6 %reduce-scatter.2.cloned.1.call-start = ((), (), s32[]{:S(2)}) async-start(), calls=%async_computation.2 | async-start | bytes 1105920 | tf_op jit(solution)/shard_map/reduce_scatter | solution.py:122
  10.2 19.7 %collective-permute-start = (bf16[256,128]{0,1:T(8,128)(2,1)}, bf16[256,128]{0,1:T(8,128)(2,1)S(1)}, u32[]{:S(2)}, u32[]{:S(2)}) collective-permute-start(bf16[256,128]{0,1:T(8,128)(2,1)} %all_gather.9), channel_id=1, source_target_pairs={{0,4},{4,8},{8,12},{12,16},{16,20},{20,24},{24,28},{1,5},{5,9},{9,... | collective-permute-start | bytes 196616 | tf_op jit(solution)/shard_map/while/body/eval_jaxpr/ppermute | solution.py:14
  17.9 12.1 %collective-permute-start.1 = (bf16[256,128]{0,1:T(8,128)(2,1)}, bf16[256,128]{0,1:T(8,128)(2,1)S(1)}, u32[]{:S(2)}, u32[]{:S(2)}) collective-permute-start(bf16[256,128]{0,1:T(8,128)(2,1)} %all_gather.10), channel_id=1, source_target_pairs={{0,4},{4,8},{8,12},{12,16},{16,20},{20,24},{24,28},{1,5},{5,9},{9,... | collective-permute-start | bytes 196616 | tf_op jit(solution)/shard_map/while/body/eval_jaxpr/ppermute | solution.py:14
  30.0 5.3 %copy-start.3 = (s32[128,4]{0,1:T(4,128)S(1)}, s32[128,4]{0,1:T(4,128)}, u32[]{:S(2)}) copy-start(s32[128,4]{0,1:T(4,128)} %param.18) | copy-start | bytes 6148
  35.3 20.5 %copy-start.2 = (bf16[128,2880]{0,1:T(8,128)(2,1)S(1)}, bf16[128,2880]{0,1:T(8,128)(2,1)}, u32[]{:S(2)}) copy-start(bf16[128,2880]{0,1:T(8,128)(2,1)} %param.12) | copy-start | bytes 2211844
  35.3 121.2 %all-gather.3.cloned.1.call-start = ((), (), s32[]{:S(2)}) async-start(), calls=%async_computation.3 | async-start | bytes 5308416 | tf_op jit(solution)/shard_map/all_gather | solution.py:143
  56.8 0.7 copy-start.1
  175.3 4.9 %copy-start = (f32[2880,576]{0,1:T(8,128)S(1)}, f32[2880,576]{0,1:T(8,128)}, u32[]{:S(2)}) copy-start(f32[2880,576]{0,1:T(8,128)} %reshape.128) | copy-start | bytes 19906564
  175.3 4.9 %copy-start.4 = (f32[2880]{0:T(1024)S(1)}, f32[2880]{0:T(1024)}, u32[]{:S(2)}) copy-start(f32[2880]{0:T(1024)} %param.17) | copy-start | bytes 34564
Sparse Core Ops, SparseCore 0:
  35.4 20.2 reduce-scatter.1
  109.2 47.2 all-gather.2
where the time goes:
time: 198 us; the launch traced here: 197 us
  waiting for transfers between devices  58 us (29%)
  blocking collectives  50.8 us (26%)
  local copies, waits for them, and re-layouts  37.9 us (19%)
  matrix products  16.6 us (8%)
  between operations  15.6 us (8%)
  other arithmetic  9.75 us (5%)
  starting transfers between devices  8.24 us (4%)
    all_to_all x1, blocking collectives, body(): lax.all_to_all(outgoing.reshape(experts_all, capacity, column_width), 'ct...  46.6 us
    all_gather x1, waiting for transfers between devices, body(): lax.all_gather(arrived_rows, 'head', axis=1, tiled=True).astype(jnp.float32)  38.5 us
    reduce_scatter x1, waiting for transfers between devices, body(): lax.psum_scatter(partial_value.astype(jnp.bfloat16), 'head', scatter_dime...  19.5 us
    convert_element_type x2, local copies, waits for them, and re-layouts, body(): lax.all_gather(arrived_rows, 'head', axis=1, tiled=True).astype(jnp.float32)  18.8 us
    unnamed x15, local copies, waits for them, and re-layouts  13.9 us
    dot_general x1, matrix products, body(): gate_up = jnp.dot(scaled, local_weight, preferred_element_type=jnp.float32)  8.21 us
    ppermute x2, starting transfers between devices, shifted(): return lax.ppermute(value, axis, pairs)  8.17 us
    dot_general x1, matrix products, body(): jnp.dot(attended, out_weight, preferred_element_type=jnp.float32)  5.25 us
  transfers between devices with their start and end apart: 4, of which 2 were waited for; matrix products, arithmetic and copies ran while one was open for 9% of the time, Pallas kernels for 0%

commit v1 on v0

--- a/solution.py
+++ b/solution.py
@@ -6,6 +6,27 @@
 D = 2880
 HD = 64
 TOP = 4
+
+
+def in_order(blocks, dim):
+    blocks = jnp.moveaxis(blocks, 0, dim)
+    lengths = blocks.shape
+    return blocks.reshape(*lengths[:dim], lengths[dim] * lengths[dim + 1], *lengths[dim + 2 :])
+
+
+def collected_by_bits(x, axis):
+    size, index = (lax.axis_size(axis), lax.axis_index(axis))
+    blocks, stride = (x[None], 1)
+    while stride < size:
+        other = lax.ppermute(blocks, axis, [(i, i ^ stride) for i in range(size)])
+        low = index & stride == 0
+        blocks = jnp.concatenate([jnp.where(low, blocks, other), jnp.where(low, other, blocks)])
+        stride *= 2
+    return blocks
+
+
+def doubled_up(array, axis, dim):
+    return in_order(collected_by_bits(array, axis), dim)
 
 
 def shifted(value, axis, by):
@@ -140,7 +161,7 @@
     )
     arrived_rows = arrived.reshape(-1, column_width)
     slot_total = arrived_rows.shape[0]
-    widened = lax.all_gather(arrived_rows, "head", axis=1, tiled=True).astype(jnp.float32)
+    widened = doubled_up(arrived_rows, "head", 1).astype(jnp.float32)
     scaled = (widened * norm_gain[None, :]).astype(jnp.bfloat16)
     gate_up = jnp.dot(scaled, local_weight, preferred_element_type=jnp.float32)
     squares = jnp.sum(widened * widened, axis=1)

time: 198 us -> 178 us (0.90)
  local copies, waits for them, and re-layouts: 37.9 us -> 27.8 us
  waiting for transfers between devices: 58 us -> 49 us
    all_gather x1 -> x0, waiting for transfers between devices: 38.5 us -> none  [body(): lax.all_gather(arrived_rows, 'head', axis=1, tiled=True).astype(jnp.float32)]
    ppermute x0 -> x1, waiting for transfers between devices: none -> 29.3 us  [collected_by_bits(): other = lax.ppermute(blocks, axis, [(i, i ^ stride) for i in range(size)])]
    convert_element_type x2, local copies, waits for them, and re-layouts: 18.8 us -> 7.89 us  [body(): scaled = (widened * norm_gain[None, :]).astype(jnp.bfloat16)]
    reduce_sum x1, other arithmetic: 3.61 us -> 1.5 us  [body(): squares = jnp.sum(widened * widened, axis=1)]
    unnamed x15 -> x11, local copies, waits for them, and re-layouts: 13.9 us -> 12.2 us
  transfers between devices with their start and end apart: 4 -> 4, of which waited for: 2 -> 2; matrix products, arithmetic and copies ran while one was open for 9% -> 10% of each run, Pallas kernels for 0% -> 0%
where the time goes in v1:
time: 178 us; the launch traced here: 177 us
  blocking collectives  50.6 us (28%)
  waiting for transfers between devices  49 us (28%)
  local copies, waits for them, and re-layouts  27.8 us (16%)
  matrix products  17.5 us (10%)
  between operations  15.6 us (9%)
  starting transfers between devices  8.77 us (5%)
  other arithmetic  7.86 us (4%)
    all_to_all x1, blocking collectives, body(): lax.all_to_all(outgoing.reshape(experts_all, capacity, column_width), 'ct...  46.5 us
    ppermute x1, waiting for transfers between devices, collected_by_bits(): other = lax.ppermute(blocks, axis, [(i, i ^ stride) for i in range(size)])  29.3 us
    reduce_scatter x1, waiting for transfers between devices, body(): lax.psum_scatter(partial_value.astype(jnp.bfloat16), 'head', scatter_dime...  19.6 us
    unnamed x11, local copies, waits for them, and re-layouts  12.2 us
    dot_general x1, matrix products, body(): gate_up = jnp.dot(scaled, local_weight, preferred_element_type=jnp.float32)  9.15 us
    ppermute x2, starting transfers between devices, shifted(): return lax.ppermute(value, axis, pairs)  8.17 us
    convert_element_type x2, local copies, waits for them, and re-layouts, body(): scaled = (widened * norm_gain[None, :]).astype(jnp.bfloat16)  7.89 us
    dot_general x1, matrix products, body(): jnp.dot(attended, out_weight, preferred_element_type=jnp.float32)  5.24 us
  transfers between devices with their start and end apart: 4, of which 2 were waited for; matrix products, arithmetic and copies ran while one was open for 10% of the time, Pallas kernels for 0%

profile of v1, /device:TPU:0, one launch (start us, length us, event | category | flops | bytes accessed | tf_op | source)
XLA Modules:
  0.0 177.1 jit_solution(11184137020403830586)
XLA Ops:
  7.2 0.0 reduce-scatter.2.cloned.1.call-start
  7.2 0.9 copy.28
  8.1 2.2 %all_gather.7 = bf16[256,128]{0,1:T(8,128)(2,1)} all-gather(bf16[128,128]{0,1:T(8,128)(2,1)S(1)} %copy.28), channel_id=1, replica_groups=mesh['ctx'=8,'grp'=2,'head'=2] {'grp'}, dimensions={0}, use_global_device_ids=true | all-gather | bytes 98304 | tf_op jit(solution)/shard_map/all_gather | solution.py:93
  10.2 4.7 %collective-permute-start.1 = (bf16[256,128]{0,1:T(8,128)(2,1)}, bf16[256,128]{0,1:T(8,128)(2,1)S(1)}, u32[]{:S(2)}, u32[]{:S(2)}) collective-permute-start(bf16[256,128]{0,1:T(8,128)(2,1)} %all_gather.7), channel_id=1, source_target_pairs={{0,4},{4,8},{8,12},{12,16},{16,20},{20,24},{24,28},{1,5},{5,9},{9,... | collective-permute-start | bytes 196616 | tf_op jit(solution)/shard_map/while/body/eval_jaxpr/ppermute | solution.py:35
  15.0 0.9 copy.26
  15.9 2.0 %all_gather.6 = bf16[256,128]{0,1:T(8,128)(2,1)} all-gather(bf16[128,128]{0,1:T(8,128)(2,1)S(1)} %copy.26), channel_id=1, replica_groups=mesh['ctx'=8,'grp'=2,'head'=2] {'grp'}, dimensions={0}, use_global_device_ids=true | all-gather | bytes 98304 | tf_op jit(solution)/shard_map/all_gather | solution.py:92
  17.9 3.4 %collective-permute-start = (bf16[256,128]{0,1:T(8,128)(2,1)}, bf16[256,128]{0,1:T(8,128)(2,1)S(1)}, u32[]{:S(2)}, u32[]{:S(2)}) collective-permute-start(bf16[256,128]{0,1:T(8,128)(2,1)} %all_gather.6), channel_id=1, source_target_pairs={{0,4},{4,8},{8,12},{12,16},{16,20},{20,24},{24,28},{1,5},{5,9},{9,... | collective-permute-start | bytes 196616 | tf_op jit(solution)/shard_map/while/body/eval_jaxpr/ppermute | solution.py:35
  21.4 0.8 fusion.46
  23.5 1.1 copy.27
  24.6 5.3 %conditional.2 = (f32[2,8,128]{2,1,0:T(8,128)}, f32[2,8,128]{2,1,0:T(8,128)S(1)}, f32[2,8,128,64]{2,3,1,0:T(8,128)S(1)}) conditional(s32[]{:T(128)} %convert_element_type.74, () %tuple.30, (pred[128,256]{0,1:T(8,128)(4,1)S(1)}, bf16[256,128]{0,1:T(8,128)(2,1)}, bf16[128,2,8,64]{0,3,2,1:T(8,128)(2,1)S(1)}, bf16[256,128]{0,1:T(8,128)(2,1)}) %tuple.54), branch_computations={%region_2.3_spmd, %region_3.6_spmd} | conditional | flops 141172736 | bytes 7397400 | solution.py:66
  24.6 1.3 fusion
  26.0 0.6 exponential_multiply_fusion
  26.6 1.2 fusion.2
  27.8 1.4 convolution_add_fusion
  29.2 0.7 fusion.11
  29.9 0.0 collective-permute-done.1
  29.9 0.0 collective-permute-done
  30.0 0.1 divide_convert_fusion
  30.0 0.0 copy-start.2
  30.0 5.2 %convolution_convert_fusion = bf16[128,2880]{0,1:T(8,128)(2,1)} fusion(bf16[1024,2880]{0,1:T(8,128)(2,1)} %param.16, bf16[128,1024]{0,1:T(8,128)(2,1)S(1)} %bitcast.78), kind=kOutput, calls=%fused_computation.36 | convolution fusion | flops 755343360 | bytes 6897664 | tf_op jit(solution)/shard_map/dot_general | solution.py:129
  35.3 0.0 copy-start.1
  35.3 0.0 reduce-scatter.2.cloned.1.call-update
  35.3 0.0 copy-done.2
  35.3 0.1 copy.30
  35.4 0.1 copy.29
  35.6 0.1 mul.114
  35.7 0.1 eq.19
  35.8 0.3 fusion.29
  36.2 19.6 %reduce-scatter.2.cloned.1.call-done = bf16[128,1440]{0,1:T(8,128)(2,1)} async-done(((bf16[128,2880]{0,1:T(8,128)(2,1)}), bf16[128,1440]{0,1:T(8,128)(2,1)}) %reduce-scatter.2.cloned.1.call-update) | async-done | bytes 368656 | tf_op jit(solution)/shard_map/reduce_scatter | solution.py:143
  55.8 0.0 copy-done.1
  55.8 1.1 add_convert_fusion
  56.9 0.0 copy-start
  56.9 0.7 copy-done
  57.6 0.2 copy.31
  57.8 0.4 broadcast_in_dim.79
  58.2 1.7 reshape.124
  59.9 4.3 %scatter_custom_fusion = bf16[576,1440]{1,0:T(8,128)(2,1)S(1)} fusion(s32[512]{0:T(512)S(1)} %bitcast.81, bf16[512,1440]{1,0:T(8,128)(2,1)} %reshape.124, bf16[]{:T(256)} %constant.51.clone.1), kind=kCustom, calls=%fused_computation.50 | custom fusion | bytes 1659392 | tf_op jit(solution)/shard_map/scatter | solution.py:153
  64.2 46.5 %all_to_all.12 = bf16[8,72,1440]{2,1,0:T(8,128)(2,1)S(1)} all-to-all(bf16[8,72,1440]{2,1,0:T(8,128)(2,1)S(1)} %bitcast.75), channel_id=1, replica_groups=mesh['ctx'=8,'grp'=2,'head'=2] {'ctx'}, dimensions={0} | all-to-all | bytes 3317760 | tf_op jit(solution)/shard_map/all_to_all | solution.py:155
  110.7 0.6 collective-permute-start.2
  111.2 0.8 mul.116
  112.0 8.5 %copy.39 = bf16[360,8,2,768]{3,1,2,0:T(8,128)(2,1)} copy(bf16[360,8,2,768]{3,2,1,0:T(2,128)(2,1)} %bitcast.71) | data formatting | bytes 17694720
  120.5 29.3 %collective-permute-done.2 = bf16[1,576,1440]{2,1,0:T(8,128)(2,1)S(1)} collective-permute-done((bf16[1,576,1440]{2,1,0:T(8,128)(2,1)S(1)}, bf16[1,576,1440]{2,1,0:T(8,128)(2,1)S(1)}, u32[]{:S(2)}, u32[]{:S(2)}) %collective-permute-start.2) | collective-permute-done | bytes 1658912 | tf_op jit(solution)/shard_map/ppermute | solution.py:21
  149.8 0.2 broadcast_select_fusion.1
  150.1 1.5 fusion.24
  151.6 3.6 %copy.32 = bf16[576,2,1440]{2,1,0:T(2,128)(2,1)S(1)} copy(bf16[576,2,1440]{2,0,1:T(8,128)(2,1)S(1)} %get-tuple-element.110) | data formatting | bytes 6635520 | tf_op jit(solution)/shard_map/convert_element_type | solution.py:165
  155.3 4.2 %convert_element_type.88 = bf16[576,2880]{1,0:T(8,128)(2,1)} reshape(bf16[576,2,1440]{2,1,0:T(2,128)(2,1)S(1)} %copy.32) | data formatting | bytes 6635520 | tf_op jit(solution)/shard_map/convert_element_type | solution.py:165
  159.5 9.2 %fusion.48 = f32[576,1536]{1,0:T(8,128)S(1)} fusion(bf16[576,2880]{1,0:T(8,128)(2,1)} %convert_element_type.88, bf16[2880,1536]{1,0:T(8,128)(2,1)} %bitcast.72), kind=kOutput, calls=%fused_computation.80 | convolution fusion | flops 5096079360 | bytes 15704064 | tf_op jit(solution)/shard_map/dot_general | solution.py:166
  168.7 1.6 fusion.33
  (9 shorter events, 0.1 us)
Async XLA Ops:
  7.2 48.6 %reduce-scatter.2.cloned.1.call-start = ((), (), s32[]{:S(2)}) async-start(), calls=%async_computation.2 | async-start | bytes 1105920 | tf_op jit(solution)/shard_map/reduce_scatter | solution.py:143
  10.2 19.7 %collective-permute-start.1 = (bf16[256,128]{0,1:T(8,128)(2,1)}, bf16[256,128]{0,1:T(8,128)(2,1)S(1)}, u32[]{:S(2)}, u32[]{:S(2)}) collective-permute-start(bf16[256,128]{0,1:T(8,128)(2,1)} %all_gather.7), channel_id=1, source_target_pairs={{0,4},{4,8},{8,12},{12,16},{16,20},{20,24},{24,28},{1,5},{5,9},{9,... | collective-permute-start | bytes 196616 | tf_op jit(solution)/shard_map/while/body/eval_jaxpr/ppermute | solution.py:35
  17.9 12.1 %collective-permute-start = (bf16[256,128]{0,1:T(8,128)(2,1)}, bf16[256,128]{0,1:T(8,128)(2,1)S(1)}, u32[]{:S(2)}, u32[]{:S(2)}) collective-permute-start(bf16[256,128]{0,1:T(8,128)(2,1)} %all_gather.6), channel_id=1, source_target_pairs={{0,4},{4,8},{8,12},{12,16},{16,20},{20,24},{24,28},{1,5},{5,9},{9,... | collective-permute-start | bytes 196616 | tf_op jit(solution)/shard_map/while/body/eval_jaxpr/ppermute | solution.py:35
  30.0 5.3 %copy-start.2 = (s32[128,4]{0,1:T(4,128)S(1)}, s32[128,4]{0,1:T(4,128)}, u32[]{:S(2)}) copy-start(s32[128,4]{0,1:T(4,128)} %param.18) | copy-start | bytes 6148
  35.3 20.5 %copy-start.1 = (bf16[128,2880]{0,1:T(8,128)(2,1)S(1)}, bf16[128,2880]{0,1:T(8,128)(2,1)}, u32[]{:S(2)}) copy-start(bf16[128,2880]{0,1:T(8,128)(2,1)} %param.12) | copy-start | bytes 2211844
  56.9 0.7 copy-start
  110.7 39.2 %collective-permute-start.2 = (bf16[1,576,1440]{2,1,0:T(8,128)(2,1)S(1)}, bf16[1,576,1440]{2,1,0:T(8,128)(2,1)S(1)}, u32[]{:S(2)}, u32[]{:S(2)}) collective-permute-start(bf16[1,576,1440]{2,1,0:T(8,128)(2,1)S(1)} %bitcast.73), channel_id=1, source_target_pairs={{0,1},{1,0},{2,3},{3,2},{4,5},{5,4},{6,7},{7,6},{8,9},{9,8},{10,11... | collective-permute-start | bytes 4976648 | tf_op jit(solution)/shard_map/ppermute | solution.py:21
Sparse Core Ops, SparseCore 0:
  35.4 20.2 reduce-scatter.1
